TPU v7x, 512 devices: a whole 4x4x16 slice. The times are simulated.
512 devices in a mesh: mem: 128 (over x, z, core), rep: 4 (over y).
Axes of the slice: x: 4, y: 4, z: 16, core: 2. Of those that a mesh axis runs over, the one named last changes fastest.
Arguments:
- states: bfloat16 [2048, 384], P('rep'), may hold values from -6 to 6
- batch_index: int32 [2, 2048], P(None, 'rep'), may hold values from 0 to 511
- obs_pick: int32 [2, 128], replicated, may hold values from 0 to 383
- norm_gain: float32 [384], replicated, may hold values from 0.5 to 1.5
- w_in: bfloat16 [384, 1024], replicated, may hold values from -0.3125 to 0.3125
- b_in: float32 [1024], replicated, may hold values from -0.5 to 0.5
- member_params: bfloat16 [128, 393216], P('mem', 'rep'), may hold values from -6 to 6
- observed: bfloat16 [2, 2048, 128], P(None, 'rep'), may hold values from -6 to 6
- perturbation: bfloat16 [128, 2, 2048, 128], P('mem', None, 'rep'), may hold values from -6 to 6
- inv_sigma: float32 [2, 2048, 128], P(None, 'rep'), may hold values from 0.5 to 4
Outputs:
- updated_params: bfloat16 [128, 393216], P('mem', 'rep')
Inputs may be any that keep to these rules, and one draw needn't show every extreme that they name: `batch_index`: row number of a start state inside the block of 512 given states that belongs to its block of 512 batch rows. `obs_pick`: observed feature numbers; a number may repeat.
All inputs are finite; a program needn't handle non-finite values.
Results may differ from a plain program's by a relative error of at most 0.0056.
Values may be sent and summed in bfloat16 or wider, within the bound.
No kernel may reach another device: no remote copies, remote signals or barrier semaphores. Data moves between devices by JAX's collectives and lax.ppermute only.
A program may use at most 64 MiB of HBM per device.

v0:
```python
import jax
import jax.numpy as jnp
from jax import lax
from jax.sharding import PartitionSpec as P

EPS = 1e-06
DT = 0.5


def hidden_layer(state, norm_gain, w_in, b_in):
    normed = (
        state * lax.rsqrt(jnp.mean(state * state, axis=-1, keepdims=True) + EPS) * norm_gain
    ).astype(jnp.bfloat16)
    return jax.nn.gelu(jnp.dot(normed, w_in, preferred_element_type=jnp.float32) + b_in).astype(
        jnp.bfloat16
    )


def member_sums(pieces):
    weighted, misfit_w = pieces
    count = weighted.shape[0]
    gram_list = []
    innov_list = []
    for item_index in range(weighted.shape[1]):
        flat = weighted[:, item_index].reshape(count, -1).astype(jnp.float32)
        anomaly = (flat - jnp.mean(flat, axis=0)).astype(jnp.bfloat16)
        misfit_flat = misfit_w[:, item_index].reshape(count, -1)
        gram_list.append(
            lax.dot_general(
                anomaly, anomaly, (((1,), (1,)), ((), ())), preferred_element_type=jnp.float32
            )
        )
        innov_list.append(
            lax.dot_general(
                anomaly, misfit_flat, (((1,), (1,)), ((), ())), preferred_element_type=jnp.float32
            )
        )
    return (jnp.stack(gram_list, axis=0), jnp.stack(innov_list, axis=0))


def solve_columns(system, right_side):
    lower_factor = jnp.linalg.cholesky(system)
    halfway = lax.linalg.triangular_solve(lower_factor, right_side, left_side=True, lower=True)
    return lax.linalg.triangular_solve(
        lower_factor, halfway, left_side=True, lower=True, transpose_a=True
    )


def on_device(
    states,
    batch_index,
    obs_pick,
    norm_gain,
    w_in,
    b_in,
    member_params,
    observed,
    perturbation,
    inv_sigma,
):
    local_members = member_params.shape[0]
    width = w_in.shape[1]
    features = w_in.shape[0]
    step_count = batch_index.shape[0]
    picked = obs_pick.shape[1]
    whole_params = lax.all_gather(member_params, "rep", axis=1, tiled=True)
    weights = whole_params.reshape(local_members, width, features)
    step_scale = DT * width ** (-0.5)
    start_state = jnp.take(states, batch_index, axis=0).astype(jnp.float32)
    shared = hidden_layer(start_state, norm_gain, w_in, b_in)
    current = start_state[None] + step_scale * jnp.einsum(
        "kbh,jhs->jkbs", shared, weights, preferred_element_type=jnp.float32
    )
    layer = hidden_layer(current, norm_gain, w_in, b_in)
    current = current + step_scale * jnp.einsum(
        "jkbh,jhs->jkbs", layer, weights, preferred_element_type=jnp.float32
    )
    feature_ids = lax.broadcasted_iota(jnp.int32, (step_count, features, picked), 1)
    selector = (feature_ids == obs_pick[:, None, :]).astype(jnp.float32)
    predicted = jnp.einsum("jkbs,ksf->jkbf", current, selector, precision=lax.Precision.HIGHEST)
    weighted = (predicted * inv_sigma).astype(jnp.bfloat16)
    misfit_w = (
        observed.astype(jnp.float32) * inv_sigma
        + perturbation.astype(jnp.float32)
        - predicted * inv_sigma
    ).astype(jnp.bfloat16)
    misfit_local = jnp.sum(jnp.square(misfit_w.astype(jnp.float32)))
    gram_items, innov_items = member_sums(
        (
            lax.all_to_all(weighted, "mem", split_axis=2, concat_axis=0, tiled=True),
            lax.all_to_all(misfit_w, "mem", split_axis=2, concat_axis=0, tiled=True),
        )
    )
    gram_matrix = jnp.sum(gram_items, axis=0)
    innovation = jnp.sum(innov_items, axis=0)
    members = gram_matrix.shape[0]
    entries = members * step_count * batch_index.shape[1] * lax.axis_size("rep") * picked
    identity = jnp.eye(members, dtype=jnp.float32)
    gram_matrix, innovation, misfit_total = lax.psum(
        (gram_matrix, innovation, misfit_local), ("mem", "rep")
    )
    system = gram_matrix + (1.0 + misfit_total / entries) * (members - 1) * identity
    coefficients = solve_columns(system, innovation)
    param_block = lax.all_to_all(member_params, "mem", split_axis=1, concat_axis=0, tiled=True)
    params_f = param_block.astype(jnp.float32)
    spread = params_f - jnp.mean(params_f, axis=0)
    change = jnp.einsum("kj,kp->jp", coefficients, spread, precision=lax.Precision.HIGHEST)
    renewed = (params_f + change).astype(jnp.bfloat16)
    return lax.all_to_all(renewed, "mem", split_axis=0, concat_axis=1, tiled=True)


def solution(mesh):
    placed = (
        P("rep", None),
        P(None, "rep"),
        P(),
        P(),
        P(),
        P(),
        P("mem", "rep"),
        P(None, "rep", None),
        P("mem", None, "rep", None),
        P(None, "rep", None),
    )
    return jax.shard_map(
        on_device, mesh=mesh, in_specs=placed, out_specs=P("mem", "rep"), check_vma=False
    )
```

profile of v0, /device:TPU:8, one launch (start us, length us, event | category | flops | bytes accessed | tf_op | source)
XLA Modules:
  0.0 755.3 jit_solution(18304707724078509563)
XLA Ops:
  6.5 0.6 broadcast.183
  7.1 2.8 reduce.16
  9.9 0.7 reshape.213
  10.6 20.2 %all-to-all-start = ((bf16[128,2,384]{2,1,0:T(2,128)(2,1)}), bf16[128,2,384]{2,1,0:T(2,128)(2,1)}, u32[]{:S(2)}, u32[]{:S(2)}) async-start(bf16[128,2,384]{2,1,0:T(2,128)(2,1)} %reshape.213), calls=%async_computation | async-start | bytes 393216 | tf_op jit(solution)/shard_map/all_to_all | solution.py:104
  30.9 0.7 fusion.75
  31.5 0.7 compare_and_fusion
  32.2 17.5 %all_gather.3 = bf16[1,393216]{1,0:T(2,128)(2,1)S(1)} all-gather(bf16[1,98304]{1,0:T(2,128)(2,1)S(1)} %copy-done.2), channel_id=1, replica_groups=mesh['mem'=128,'rep'=4] {'rep'}, dimensions={1}, use_global_device_ids=true | all-gather | bytes 983040 | tf_op jit(solution)/shard_map/all_gather | solution.py:66
  49.8 16.3 %reduce.14 = bf16[393216]{0:T(1024)(128)(2,1)S(1)} reduce(bf16[1,393216]{1,0:T(2,128)(2,1)S(1)} %all_gather.3, bf16[]{:T(256)} %constant.98), dimensions={0}, to_apply=%all_gather.3.reduce_sub_computation | reduce | bytes 1572866 | tf_op jit(solution)/shard_map/all_gather | solution.py:66
  66.1 1.2 reshape.185
  67.4 1.3 reshape.205
  68.6 4.1 gather_fusion
  72.8 0.4 fusion.16
  73.2 1.2 copy.38
  74.4 4.1 multiply_reduce_fusion
  78.6 1.2 copy.43
  79.9 0.1 copy.50
  80.0 1.8 copy.52
  81.8 5.2 fusion.25
  87.0 3.7 multiply_reduce_fusion.1
  90.7 1.8 copy.44
  92.5 16.3 %all-to-all-start.1 = ((bf16[1,2,512,128]{3,1,0,2:T(2,128)(2,1)}), bf16[1,2,512,128]{3,1,0,2:T(2,128)(2,1)S(1)}, u32[]{:S(2)}, u32[]{:S(2)}) async-start(bf16[1,2,512,128]{3,1,0,2:T(2,128)(2,1)} %copy.44), calls=%async_computation.1 | async-start | bytes 524288 | tf_op jit(solution)/shard_map/all_to_all | solution.py:90
  108.8 0.9 copy.54
  109.7 22.9 %all-to-all-done.1 = bf16[1,2,512,128]{3,1,0,2:T(2,128)(2,1)S(1)} async-done(((bf16[1,2,512,128]{3,1,0,2:T(2,128)(2,1)}), bf16[1,2,512,128]{3,1,0,2:T(2,128)(2,1)S(1)}, u32[]{:S(2)}, u32[]{:S(2)}) %all-to-all-start.1) | async-done | bytes 262176 | tf_op jit(solution)/shard_map/all_to_all | solution.py:90
  132.6 6.2 all-to-all-start.2
  138.7 0.0 all-reduce.3.cloned.1.call-start
  138.8 105.2 %psum.22 = f32[]{:T(128)} all-reduce(f32[]{:T(128)} %get-tuple-element.9), channel_id=1, replica_groups=mesh['mem'=128,'rep'=4] {'mem','rep'}, use_global_device_ids=true, to_apply=%region_6.7 | all-reduce | flops 1 | bytes 8 | tf_op jit(solution)/shard_map/psum | solution.py:99
  244.6 1.6 reshape.214
  246.3 0.1 convert_reduce_fusion.2
  246.5 0.1 fusion.63
  246.6 0.2 convolution_bitcast_fusion.2
  246.8 0.2 convolution_bitcast_fusion
  247.0 0.8 fusion.31
  247.8 0.8 fusion.32
  248.7 442.5 %all-reduce.3.cloned.1.call-done = (f32[128,128]{1,0:T(8,128)}, f32[128,128]{1,0:T(8,128)}) async-done(((f32[128,128]{1,0:T(8,128)}, f32[128,128]{1,0:T(8,128)}), (f32[128,128]{1,0:T(8,128)}, f32[128,128]{1,0:T(8,128)})) %all-reduce.3.cloned.1.call-update) | async-done | bytes 131088 | tf_op jit(solution)/shard_map/psum | solution.py:99
  691.2 0.9 select_add_fusion
  692.1 0.1 copy.53
  692.2 0.9 fusion.74
  693.0 11.7 %cholesky.16 = f32[128,128]{1,0:T(8,128)S(1)} custom-call(f32[128,128]{1,0:T(8,128)S(1)} %fusion.74), custom_call_target="Cholesky" | custom-call | tf_op jit(solution)/shard_map/jit(cholesky)/cholesky | solution.py:42
  704.8 0.6 compare_reduce_fusion
  705.4 0.7 fusion.69
  706.1 9.8 %custom-call.8 = f32[1,128,128]{1,2,0:T(8,128)S(1)} custom-call(f32[1,128,128]{2,1,0:T(8,128)S(1)} %fusion.69), custom_call_target="InvertDiagBlocksLowerTriangular" | custom-call | tf_op jit(solution)/shard_map/triangular_solve | solution.py:44
  715.9 1.1 fusion.72
  717.0 0.2 fusion.70
  717.2 0.5 fusion.30
  717.8 0.8 reduce.17
  718.5 0.1 reshape.215
  718.6 28.9 %all_to_all.65 = bf16[128,2,384]{2,1,0:T(2,128)(2,1)S(1)} all-to-all(bf16[128,2,384]{2,1,0:T(2,128)(2,1)S(1)} %reshape.215), channel_id=1, replica_groups=mesh['mem'=128,'rep'=4] {'mem'}, dimensions={0} | all-to-all | bytes 393216 | tf_op jit(solution)/shard_map/all_to_all | solution.py:109
  747.5 0.9 reshape.216
  (27 shorter events, 0.2 us)
Async XLA Ops:
  6.5 67.9 %copy-start = (bf16[384,1024]{1,0:T(8,128)(2,1)S(1)}, bf16[384,1024]{1,0:T(8,128)(2,1)}, u32[]{:S(2)}) copy-start(bf16[384,1024]{1,0:T(8,128)(2,1)} %param.14) | copy-start | bytes 2359300
  6.5 25.7 %copy-start.2 = (bf16[1,98304]{1,0:T(2,128)(2,1)S(1)}, bf16[1,98304]{1,0:T(2,128)(2,1)}, u32[]{:S(2)}) copy-start(bf16[1,98304]{1,0:T(2,128)(2,1)} %param.16) | copy-start | bytes 589828
  10.6 81.9 %all-to-all-start = ((bf16[128,2,384]{2,1,0:T(2,128)(2,1)}), bf16[128,2,384]{2,1,0:T(2,128)(2,1)}, u32[]{:S(2)}, u32[]{:S(2)}) async-start(bf16[128,2,384]{2,1,0:T(2,128)(2,1)} %reshape.213), calls=%async_computation | async-start | bytes 393216 | tf_op jit(solution)/shard_map/all_to_all | solution.py:104
  66.1 2.5 copy-start.1
  72.7 1.7 copy-start.5
  72.7 1.7 copy-start.6
  74.4 5.4 copy-start.3
  81.8 5.2 copy-start.4
  92.5 40.0 %all-to-all-start.1 = ((bf16[1,2,512,128]{3,1,0,2:T(2,128)(2,1)}), bf16[1,2,512,128]{3,1,0,2:T(2,128)(2,1)S(1)}, u32[]{:S(2)}, u32[]{:S(2)}) async-start(bf16[1,2,512,128]{3,1,0,2:T(2,128)(2,1)} %copy.44), calls=%async_computation.1 | async-start | bytes 524288 | tf_op jit(solution)/shard_map/all_to_all | solution.py:90
  132.6 114.2 %all-to-all-start.2 = ((bf16[1,2,512,128]{3,1,0,2:T(2,128)(2,1)}), bf16[1,2,512,128]{3,1,0,2:T(2,128)(2,1)S(1)}, u32[]{:S(2)}, u32[]{:S(2)}) async-start(bf16[1,2,512,128]{3,1,0,2:T(2,128)(2,1)} %copy.54), calls=%async_computation.2 | async-start | bytes 524288 | tf_op jit(solution)/shard_map/all_to_all | solution.py:91
  138.7 552.5 %all-reduce.3.cloned.1.call-start = ((), (), s32[]{:S(2)}) async-start(), calls=%async_computation.4 | async-start | bytes 262144 | tf_op jit(solution)/shard_map/psum | solution.py:99
Sparse Core Ops, SparseCore 0:
  248.8 442.3 all-reduce.2
where the time goes:
time: 756 us; the launch traced here: 755 us
  waiting for transfers between devices  465 us (62%)
  blocking collectives  152 us (20%)
  other arithmetic  46.5 us (6%)
  starting transfers between devices  42.8 us (6%)
  local copies, waits for them, and re-layouts  17.6 us (2%)
  matrix products  16.9 us (2%)
  between operations  14.3 us (2%)
    psum x1, waiting for transfers between devices, on_device(): lax.psum((gram_matrix, innovation, misfit_local), ('mem', 'rep'))  443 us
    psum x1, blocking collectives, on_device(): lax.psum((gram_matrix, innovation, misfit_local), ('mem', 'rep'))  105 us
    all_to_all x1, blocking collectives, on_device(): lax.all_to_all(renewed, 'mem', split_axis=0, concat_axis=1, tiled=True)  28.9 us
    all_to_all x1, waiting for transfers between devices, on_device(): lax.all_to_all(weighted, 'mem', split_axis=2, concat_axis=0, tiled=True)  22.9 us
    all_to_all x1, starting transfers between devices, on_device(): lax.all_to_all(member_params, 'mem', split_axis=1, concat_axis=0, tiled=T...  20.2 us
    all_gather x1, blocking collectives, on_device(): whole_params = lax.all_gather(member_params, 'rep', axis=1, tiled=True)  17.5 us
    all_gather x1, other arithmetic, on_device(): whole_params = lax.all_gather(member_params, 'rep', axis=1, tiled=True)  16.3 us
    all_to_all x1, starting transfers between devices, on_device(): lax.all_to_all(weighted, 'mem', split_axis=2, concat_axis=0, tiled=True)  16.3 us
  transfers between devices with their start and end apart: 4, of which 2 were waited for; matrix products, arithmetic and copies ran while one was open for 6% of the time, Pallas kernels for 0%

commit v1 on v0

--- a/solution.py
+++ b/solution.py
@@ -87,7 +87,12 @@
     misfit_local = jnp.sum(jnp.square(misfit_w.astype(jnp.float32)))
     gram_items, innov_items = member_sums(
         (
-            lax.all_to_all(weighted, "mem", split_axis=2, concat_axis=0, tiled=True),
+            jnp.concatenate(
+                lax.all_to_all(
+                    jnp.stack(jnp.split(weighted, lax.axis_size("mem"), axis=2)), "mem", 0, 0
+                ),
+                axis=0,
+            ),
             lax.all_to_all(misfit_w, "mem", split_axis=2, concat_axis=0, tiled=True),
         )
     )

time: 756 us -> 859 us (1.14)
  local copies, waits for them, and re-layouts: 17.6 us -> 114 us
    unnamed x23 -> x146, local copies, waits for them, and re-layouts: 7.01 us -> 97.6 us
  transfers between devices with their start and end apart: 4 -> 4, of which waited for: 2 -> 2; matrix products, arithmetic and copies ran while one was open for 6% -> 17% of each run, Pallas kernels for 0% -> 0%
where the time goes in v1:
time: 859 us; the launch traced here: 852 us
  waiting for transfers between devices  466 us (54%)
  blocking collectives  152 us (18%)
  local copies, waits for them, and re-layouts  114 us (13%)
  other arithmetic  46.6 us (5%)
  starting transfers between devices  42.8 us (5%)
  matrix products  16.2 us (2%)
  between operations  14.7 us (2%)
    psum x1, waiting for transfers between devices, on_device(): lax.psum((gram_matrix, innovation, misfit_local), ('mem', 'rep'))  443 us
    psum x1, blocking collectives, on_device(): lax.psum((gram_matrix, innovation, misfit_local), ('mem', 'rep'))  105 us
    unnamed x146, local copies, waits for them, and re-layouts  97.6 us
    all_to_all x1, blocking collectives, on_device(): lax.all_to_all(renewed, 'mem', split_axis=0, concat_axis=1, tiled=True)  28.9 us
    all_to_all x1, waiting for transfers between devices, on_device(): lax.all_to_all(jnp.stack(jnp.split(weighted, lax.axis_size('mem'), axis=2...  22.8 us
    all_to_all x1, starting transfers between devices, on_device(): lax.all_to_all(member_params, 'mem', split_axis=1, concat_axis=0, tiled=T...  20.2 us
    all_gather x1, blocking collectives, on_device(): whole_params = lax.all_gather(member_params, 'rep', axis=1, tiled=True)  17.9 us
  transfers between devices with their start and end apart: 4, of which 2 were waited for; matrix products, arithmetic and copies ran while one was open for 17% of the time, Pallas kernels for 0%

profile of v1, /device:TPU:8, one launch (start us, length us, event | category | flops | bytes accessed | tf_op | source)
XLA Modules:
  0.0 851.6 jit_solution(15369485032678634866)
XLA Ops:
  7.1 2.8 reduce.16
  9.9 0.7 reshape.217
  10.6 20.2 %all-to-all-start = ((bf16[128,2,384]{2,1,0:T(2,128)(2,1)}), bf16[128,2,384]{2,1,0:T(2,128)(2,1)}, u32[]{:S(2)}, u32[]{:S(2)}) async-start(bf16[128,2,384]{2,1,0:T(2,128)(2,1)} %reshape.217), calls=%async_computation | async-start | bytes 393216 | tf_op jit(solution)/shard_map/all_to_all | solution.py:109
  32.3 17.9 %all_gather.3 = bf16[1,393216]{1,0:T(2,128)(2,1)S(1)} all-gather(bf16[1,98304]{1,0:T(2,128)(2,1)} %param.16), channel_id=1, replica_groups=mesh['mem'=128,'rep'=4] {'rep'}, dimensions={1}, use_global_device_ids=true | all-gather | bytes 983040 | tf_op jit(solution)/shard_map/all_gather | solution.py:66
  50.2 16.3 %reduce.14 = bf16[393216]{0:T(1024)(128)(2,1)S(1)} reduce(bf16[1,393216]{1,0:T(2,128)(2,1)S(1)} %all_gather.3, bf16[]{:T(256)} %constant.98), dimensions={0}, to_apply=%all_gather.3.reduce_sub_computation | reduce | bytes 1572866 | tf_op jit(solution)/shard_map/all_gather | solution.py:66
  66.5 1.2 reshape.188
  67.7 1.3 reshape.209
  69.0 4.1 gather_fusion
  73.6 1.2 copy.190
  74.8 4.1 multiply_reduce_fusion
  78.9 1.2 copy.195
  80.1 1.1 copy.201
  81.2 1.8 copy.203
  83.0 5.2 fusion.25
  88.2 3.0 multiply_reduce_fusion.1
  94.7 0.7 constant_dynamic-update-slice_fusion.122
  96.8 0.7 constant_dynamic-update-slice_fusion.119
  101.1 0.7 constant_dynamic-update-slice_fusion.113
  101.8 0.7 constant_dynamic-update-slice_fusion.112
  111.0 0.7 constant_dynamic-update-slice_fusion.99
  113.1 0.7 constant_dynamic-update-slice_fusion.96
  121.5 0.7 constant_dynamic-update-slice_fusion.84
  123.6 0.7 constant_dynamic-update-slice_fusion.81
  132.1 0.7 constant_dynamic-update-slice_fusion.69
  147.6 0.7 constant_dynamic-update-slice_fusion.47
  150.4 0.7 constant_dynamic-update-slice_fusion.43
  152.5 0.7 constant_dynamic-update-slice_fusion.40
  166.6 0.9 constant_dynamic-update-slice_fusion.20
  178.8 0.7 constant_dynamic-update-slice_fusion.3
  180.9 0.7 constant_dynamic-update-slice_fusion
  181.6 7.0 copy.196
  188.6 16.3 %all-to-all-start.1 = ((bf16[128,1,2,4,128]{4,3,2,1,0:T(4,128)(2,1)}), bf16[128,1,2,4,128]{4,3,2,1,0:T(4,128)(2,1)S(1)}, u32[]{:S(2)}, u32[]{:S(2)}) async-start(bf16[128,1,2,4,128]{4,3,2,1,0:T(4,128)(2,1)} %copy.196), calls=%async_computation.1 | async-start | bytes 524288 | tf_op jit(solution)/shard_map/all_to_all | solution.py:91
  204.9 0.9 copy.205
  205.8 22.8 %all-to-all-done.1 = bf16[128,1,2,4,128]{4,3,2,1,0:T(4,128)(2,1)S(1)} async-done(((bf16[128,1,2,4,128]{4,3,2,1,0:T(4,128)(2,1)}), bf16[128,1,2,4,128]{4,3,2,1,0:T(4,128)(2,1)S(1)}, u32[]{:S(2)}, u32[]{:S(2)}) %all-to-all-start.1) | async-done | bytes 262176 | tf_op jit(solution)/shard_map/all_to_all | solution.py:91
  228.6 6.2 all-to-all-start.2
  234.9 105.0 %psum.22 = f32[]{:T(128)} all-reduce(f32[]{:T(128)} %get-tuple-element.9), channel_id=1, replica_groups=mesh['mem'=128,'rep'=4] {'mem','rep'}, use_global_device_ids=true, to_apply=%region_6.7 | all-reduce | flops 1 | bytes 8 | tf_op jit(solution)/shard_map/psum | solution.py:104
  340.5 1.6 reshape.218
  342.8 0.8 fusion.31
  343.6 0.8 fusion.32
  344.5 442.7 %all-reduce.3.cloned.1.call-done = (f32[128,128]{1,0:T(8,128)}, f32[128,128]{1,0:T(8,128)}) async-done(((f32[128,128]{1,0:T(8,128)}, f32[128,128]{1,0:T(8,128)}), (f32[128,128]{1,0:T(8,128)}, f32[128,128]{1,0:T(8,128)})) %all-reduce.3.cloned.1.call-update) | async-done | bytes 131088 | tf_op jit(solution)/shard_map/psum | solution.py:104
  787.2 0.9 select_add_fusion
  788.1 0.9 fusion.74
  789.0 11.7 %cholesky.16 = f32[128,128]{1,0:T(8,128)S(1)} custom-call(f32[128,128]{1,0:T(8,128)S(1)} %fusion.74), custom_call_target="Cholesky" | custom-call | tf_op jit(solution)/shard_map/jit(cholesky)/cholesky | solution.py:42
  802.0 9.8 %custom-call.8 = f32[1,128,128]{1,2,0:T(8,128)S(1)} custom-call(f32[1,128,128]{2,1,0:T(8,128)S(1)} %fusion.69), custom_call_target="InvertDiagBlocksLowerTriangular" | custom-call | tf_op jit(solution)/shard_map/triangular_solve | solution.py:44
  811.9 1.1 fusion.72
  813.7 0.8 reduce.17
  814.6 28.9 %all_to_all.52 = bf16[128,2,384]{2,1,0:T(2,128)(2,1)S(1)} all-to-all(bf16[128,2,384]{2,1,0:T(2,128)(2,1)S(1)} %reshape.219), channel_id=1, replica_groups=mesh['mem'=128,'rep'=4] {'mem'}, dimensions={0} | all-to-all | bytes 393216 | tf_op jit(solution)/shard_map/all_to_all | solution.py:114
  843.5 0.9 reshape.220
  (150 shorter events, 84.9 us)
Async XLA Ops:
  6.5 68.2 %copy-start = (bf16[384,1024]{1,0:T(8,128)(2,1)S(1)}, bf16[384,1024]{1,0:T(8,128)(2,1)}, u32[]{:S(2)}) copy-start(bf16[384,1024]{1,0:T(8,128)(2,1)} %param.14) | copy-start | bytes 2359300
  6.5 62.5 %copy-start.1 = (bf16[512,384]{1,0:T(8,128)(2,1)S(1)}, bf16[512,384]{1,0:T(8,128)(2,1)}, u32[]{:S(2)}) copy-start(bf16[512,384]{1,0:T(8,128)(2,1)} %param.10) | copy-start | bytes 1179652
  10.6 178.0 %all-to-all-start = ((bf16[128,2,384]{2,1,0:T(2,128)(2,1)}), bf16[128,2,384]{2,1,0:T(2,128)(2,1)}, u32[]{:S(2)}, u32[]{:S(2)}) async-start(bf16[128,2,384]{2,1,0:T(2,128)(2,1)} %reshape.217), calls=%async_computation | async-start | bytes 393216 | tf_op jit(solution)/shard_map/all_to_all | solution.py:109
  32.3 42.5 %copy-start.3 = (f32[1024]{0:T(1024)S(1)}, f32[1024]{0:T(1024)}, u32[]{:S(2)}) copy-start(f32[1024]{0:T(1024)} %param.15) | copy-start | bytes 12292
  32.3 42.5 %copy-start.4 = (f32[384]{0:T(512)S(1)}, f32[384]{0:T(512)}, u32[]{:S(2)}) copy-start(f32[384]{0:T(512)} %param.13) | copy-start | bytes 4612
  83.0 5.2 copy-start.2
  188.6 40.0 %all-to-all-start.1 = ((bf16[128,1,2,4,128]{4,3,2,1,0:T(4,128)(2,1)}), bf16[128,1,2,4,128]{4,3,2,1,0:T(4,128)(2,1)S(1)}, u32[]{:S(2)}, u32[]{:S(2)}) async-start(bf16[128,1,2,4,128]{4,3,2,1,0:T(4,128)(2,1)} %copy.196), calls=%async_computation.1 | async-start | bytes 524288 | tf_op jit(solution)/shard_map/all_to_all | solution.py:91
  228.6 113.9 %all-to-all-start.2 = ((bf16[1,2,512,128]{3,1,0,2:T(2,128)(2,1)}), bf16[1,2,512,128]{3,1,0,2:T(2,128)(2,1)S(1)}, u32[]{:S(2)}, u32[]{:S(2)}) async-start(bf16[1,2,512,128]{3,1,0,2:T(2,128)(2,1)} %copy.205), calls=%async_computation.2 | async-start | bytes 524288 | tf_op jit(solution)/shard_map/all_to_all | solution.py:96
  234.8 552.4 %all-reduce.3.cloned.1.call-start = ((), (), s32[]{:S(2)}) async-start(), calls=%async_computation.4 | async-start | bytes 262144 | tf_op jit(solution)/shard_map/psum | solution.py:104
Sparse Core Ops, SparseCore 0:
  344.6 442.5 all-reduce.2
